TPU v7x, 512 devices: a whole 4x4x16 slice. The times are simulated.
512 devices in a mesh: ctx: 32 (over x, z_lo), tp: 16 (over y, z_hi, core).
Axes of the slice: x: 4, y: 4, z: 16 (z_hi: 2, z_lo: 8; z = z_hi * 8 + z_lo), core: 2. Of those that a mesh axis runs over, the one named last changes fastest.
Arguments:
- queries: bfloat16 [4096, 4096], P('ctx', 'tp'), may hold values from -5 to 5
- key_states: bfloat16 [4096, 4096], P('ctx', 'tp'), may hold values from -5 to 5
- value_states: bfloat16 [4096, 4096], P('ctx', 'tp'), may hold values from -6 to 6
- attn_output: bfloat16 [4096, 4096], P('ctx', 'tp'), may hold values from -6 to 6
- output_grad: bfloat16 [4096, 4096], P('ctx', 'tp'), may hold values from -6 to 6
- block_map: int32 [32, 32], replicated, may hold values from 0 to 1, as said below
- w_query: bfloat16 [8192, 4096], P('ctx', 'tp'), may hold values from -0.09375 to 0.09375
- w_key: bfloat16 [8192, 4096], P('ctx', 'tp'), may hold values from -0.09375 to 0.09375
- w_value: bfloat16 [8192, 4096], P('ctx', 'tp'), may hold values from -0.09375 to 0.09375
Outputs:
- grad_input: bfloat16 [4096, 8192], P('tp', 'ctx')
Inputs may be any that keep to these rules, and one draw needn't show every extreme that they name: block_map[i, j] is 1 wherever |i - j| <= 1; elsewhere each row is 1 on a share of its entries that differs from row to row.
All inputs are finite; a program needn't handle non-finite values.
Results may differ from a plain program's by a relative error of at most 0.014.
Values may be sent and summed in bfloat16 or wider, within the bound.
No kernel may reach another device: no remote copies, remote signals or barrier semaphores. Data moves between devices by JAX's collectives and lax.ppermute only.
A program may use at most 64 MiB of HBM per device.

v0:
```python
import math
import jax
import jax.numpy as jnp
from jax import lax
from jax.sharding import PartitionSpec as P

HD = 128
BLK = 128
NEG_FILL = -1e30


def block_mask(block_map, row_offset, row_count, col_offset, col_count):
    tiles = lax.dynamic_slice(
        block_map, (row_offset // BLK, col_offset // BLK), (row_count // BLK, col_count // BLK)
    )
    spread = jnp.broadcast_to(
        tiles[:, None, :, None], (row_count // BLK, BLK, col_count // BLK, BLK)
    )
    return spread.reshape(row_count, col_count) > 0


def resolved_rows(values):
    return lax.optimization_barrier(values.astype(jnp.bfloat16)).astype(jnp.float32)


def stat_update(state, query_heads, key_block, allowed, score_scale):
    row_max, row_sum = state
    scores = (
        jnp.einsum("qhd,khd->hqk", query_heads, key_block, preferred_element_type=jnp.float32)
        * score_scale
    )
    masked = jnp.where(allowed[None], scores, NEG_FILL)
    new_max = jnp.maximum(row_max, jnp.max(masked, axis=2))
    kept = jnp.where(allowed[None], jnp.exp(masked - new_max[:, :, None]), 0.0)
    return (new_max, row_sum * jnp.exp(row_max - new_max) + jnp.sum(kept, axis=2))


def gradient_block(
    query_heads, grad_heads, key_block, value_block, log_total, row_delta, allowed, score_scale
):
    scores = (
        jnp.einsum("qhd,khd->hqk", query_heads, key_block, preferred_element_type=jnp.float32)
        * score_scale
    )
    masked = jnp.where(allowed[None], scores, NEG_FILL)
    probs = jnp.where(allowed[None], jnp.exp(masked - log_total[:, :, None]), 0.0)
    probs_low = probs.astype(jnp.bfloat16)
    dprobs = jnp.einsum("qhd,khd->hqk", grad_heads, value_block, preferred_element_type=jnp.float32)
    score_gradient = (probs * (dprobs - row_delta[:, :, None]) * score_scale).astype(jnp.bfloat16)
    return (probs_low, score_gradient)


def per_device(
    queries, key_states, value_states, attn_output, output_grad, block_map, w_query, w_key, w_value
):
    slab_rows, width = queries.shape
    head_count = width // HD
    context_count = lax.axis_size("ctx")
    score_scale = 1.0 / math.sqrt(HD)
    row_offset = lax.axis_index("ctx") * slab_rows
    query_heads = queries.reshape(slab_rows, head_count, HD)
    grad_heads = output_grad.reshape(slab_rows, head_count, HD)
    output_heads = attn_output.reshape(slab_rows, head_count, HD)
    row_delta = jnp.sum(grad_heads.astype(jnp.float32) * output_heads.astype(jnp.float32), axis=2).T
    start_state = (
        jnp.full((head_count, slab_rows), NEG_FILL, jnp.float32),
        jnp.zeros((head_count, slab_rows), jnp.float32),
    )
    full_keys, full_values = (
        lax.all_gather(key_states, "ctx", axis=0, tiled=True),
        lax.all_gather(value_states, "ctx", axis=0, tiled=True),
    )
    group_size = min(context_count, max(1, 512 // slab_rows))
    key_span = slab_rows * group_size
    total_block_count = context_count // group_size
    key_blocks = full_keys.reshape(total_block_count, key_span, head_count, HD)
    value_blocks = full_values.reshape(total_block_count, key_span, head_count, HD)
    block_ids = jnp.arange(total_block_count, dtype=jnp.int32)

    def stat_step(state, inputs):
        key_block, block_index = inputs
        allowed = block_mask(block_map, row_offset, slab_rows, block_index * key_span, key_span)

        def stat_active_step(previous):
            return stat_update(previous, query_heads, key_block, allowed, score_scale)

        return (
            lax.cond(jnp.any(allowed), stat_active_step, lambda previous: previous, state),
            None,
        )

    (row_max, row_sum), _ = lax.scan(stat_step, start_state, (key_blocks, block_ids))
    log_total = row_max + jnp.log(row_sum)

    def back_step(dq_total, inputs):
        key_block, value_block, block_index = inputs
        allowed = block_mask(block_map, row_offset, slab_rows, block_index * key_span, key_span)

        def back_active_step(previous):
            probs_low, score_gradient = gradient_block(
                query_heads,
                grad_heads,
                key_block,
                value_block,
                log_total,
                row_delta,
                allowed,
                score_scale,
            )
            dv_part = jnp.einsum(
                "hqk,qhd->khd", probs_low, grad_heads, preferred_element_type=jnp.float32
            ).astype(jnp.bfloat16)
            dk_part = jnp.einsum(
                "hqk,qhd->khd", score_gradient, query_heads, preferred_element_type=jnp.float32
            ).astype(jnp.bfloat16)
            per_slab = jnp.einsum(
                "hqgk,gkhd->gqhd",
                score_gradient.reshape(head_count, slab_rows, group_size, slab_rows),
                key_block.reshape(group_size, slab_rows, head_count, HD),
                preferred_element_type=jnp.float32,
            )
            joined = jnp.concatenate(
                [dk_part.reshape(key_span, width), dv_part.reshape(key_span, width)], axis=1
            )
            return (previous + jnp.sum(resolved_rows(per_slab), axis=0), joined)

        def empty_step(previous):
            return (previous, jnp.zeros((key_span, 2 * width), jnp.bfloat16))

        return lax.cond(jnp.any(allowed), back_active_step, empty_step, dq_total)

    dq_total, joined_blocks = lax.scan(
        back_step,
        jnp.zeros((slab_rows, head_count, HD), jnp.float32),
        (key_blocks, value_blocks, block_ids),
    )
    local_grads = dq_total.astype(jnp.bfloat16).reshape(slab_rows, width)
    part_grads = joined_blocks.reshape(context_count * slab_rows, 2 * width)
    part_width = part_grads.shape[1]
    arrived = lax.all_to_all(
        part_grads.reshape(context_count, slab_rows, part_width),
        "ctx",
        split_axis=0,
        concat_axis=0,
        tiled=True,
    )
    finished = jnp.sum(arrived.astype(jnp.float32), axis=0).astype(jnp.bfloat16)
    own_grads = jnp.concatenate([local_grads, finished], axis=1)
    gradients = lax.all_gather(own_grads, "ctx", axis=0, tiled=True)
    projections = jnp.concatenate([w_query, w_key, w_value], axis=1)
    return lax.psum_scatter(
        lax.dot_general(
            gradients, projections, (((1,), (1,)), ((), ())), preferred_element_type=jnp.float32
        ).astype(jnp.bfloat16),
        "tp",
        scatter_dimension=0,
        tiled=True,
    )


def solution(mesh):
    return jax.shard_map(
        per_device,
        mesh=mesh,
        in_specs=(
            P("ctx", "tp"),
            P("ctx", "tp"),
            P("ctx", "tp"),
            P("ctx", "tp"),
            P("ctx", "tp"),
            P(),
            P("ctx", "tp"),
            P("ctx", "tp"),
            P("ctx", "tp"),
        ),
        out_specs=P("tp", "ctx"),
        check_vma=False,
    )
```

profile of v0, /device:TPU:2, one launch (start us, length us, event | category | flops | bytes accessed | tf_op | source)
XLA Modules:
  0.0 1083.6 jit_solution(8561882724283096852)
XLA Ops:
  8.0 1.0 copy.66
  9.1 1.0 copy.70
  10.1 0.9 copy.71
  11.1 212.4 %all-gather.4.cloned.1.call-done = bf16[4096,256]{1,0:T(8,128)(2,1)} async-done(((bf16[128,256]{1,0:T(8,128)(2,1)}), bf16[4096,256]{1,0:T(8,128)(2,1)}) %all-gather.4.cloned.1.call-update) | async-done | bytes 2097168 | tf_op jit(solution)/shard_map/all_gather | solution.py:70
  223.4 4.0 reshape.84
  227.4 2.0 copy.72
  229.5 30.8 %while.33 = (s32[]{:T(128)}, f32[2,128]{1,0:T(2,128)S(1)}, f32[2,128]{1,0:T(2,128)S(1)}, s32[8]{0:T(128)S(1)}, s32[32,32]{1,0:T(8,128)}, /*index=5*/s32[]{:T(128...) while((s32[]{:T(128)}, f32[2,128]{1,0:T(2,128)S(1)}, ...), condition=%wide.region_6.7_spmd, body=%wide.region_0.6_spmd.sunk | while | flops 34406940 | bytes 1391623 | solution.py:92
  230.6 0.8 broadcast_compare_fusion.6
  231.4 0.8 broadcast_reduce_fusion.4
  234.5 0.8 broadcast_compare_fusion.6
  235.3 0.8 broadcast_reduce_fusion.4
  238.3 0.8 broadcast_compare_fusion.6
  239.1 0.8 broadcast_reduce_fusion.4
  242.2 0.8 broadcast_compare_fusion.6
  243.0 0.8 broadcast_reduce_fusion.4
  246.0 0.8 broadcast_compare_fusion.6
  246.8 0.8 broadcast_reduce_fusion.4
  249.9 0.8 broadcast_compare_fusion.6
  250.7 0.8 broadcast_reduce_fusion.4
  253.8 0.8 broadcast_compare_fusion.6
  257.6 0.8 broadcast_compare_fusion.6
  260.3 189.8 %all-gather.6.cloned.1.call-done = bf16[4096,256]{1,0:T(8,128)(2,1)} async-done(((bf16[128,256]{1,0:T(8,128)(2,1)}), bf16[4096,256]{1,0:T(8,128)(2,1)}) %all-gather.6.cloned.1.call-update) | async-done | bytes 2097168 | tf_op jit(solution)/shard_map/all_gather | solution.py:71
  450.1 4.0 reshape.85
  454.1 3.3 copy.73
  457.5 54.5 %while.34 = (s32[]{:T(128)}, f32[128,2,128]{2,0,1:T(8,128)S(1)}, bf16[8,512,512]{2,1,0:T(8,128)(2,1)}, s32[8]{0:T(128)S(1)}, s32[32,32]{1,0:T(8,128)}, /*index=5...) while((s32[]{:T(128)}, f32[128,2,128]{2,0,1:T(8,128)S(1)}, ...), condition=%wide.region_13.14_spmd, body=%wide.region_8.13_spmd.sunk | while | flops 170721312 | bytes 8655399 | solution.py:132
  458.6 0.8 broadcast_compare_fusion.7
  460.7 2.5 conditional.5
  461.2 1.2 fusion.11
  463.4 0.8 constant_dynamic-update-slice_fusion.2
  465.4 0.8 broadcast_compare_fusion.7
  467.5 2.5 conditional.5
  468.0 1.2 fusion.11
  470.2 0.8 constant_dynamic-update-slice_fusion.2
  472.2 0.8 broadcast_compare_fusion.7
  474.3 2.5 conditional.5
  474.8 1.2 fusion.11
  477.0 0.8 constant_dynamic-update-slice_fusion.2
  479.1 0.8 broadcast_compare_fusion.7
  481.2 2.5 conditional.5
  481.6 1.2 fusion.11
  483.9 0.8 constant_dynamic-update-slice_fusion.2
  485.9 0.8 broadcast_compare_fusion.7
  488.0 2.5 conditional.5
  488.4 1.2 fusion.11
  490.7 0.8 constant_dynamic-update-slice_fusion.2
  492.7 0.8 broadcast_compare_fusion.7
  493.4 0.8 broadcast_reduce_fusion.5
  494.8 2.5 conditional.5
  495.2 1.2 fusion.11
  497.5 0.9 constant_dynamic-update-slice_fusion.2
  499.5 0.8 broadcast_compare_fusion.7
  501.6 2.5 conditional.5
  502.0 1.2 fusion.11
  504.3 0.8 constant_dynamic-update-slice_fusion.2
  506.3 0.8 broadcast_compare_fusion.7
  508.4 2.5 conditional.5
  508.8 1.2 fusion.11
  511.1 0.8 constant_dynamic-update-slice_fusion.2
  511.9 30.9 %all-to-all-start = ((bf16[32,128,512]{2,1,0:T(8,128)(2,1)}), bf16[32,128,512]{2,1,0:T(8,128)(2,1)}, u32[]{:S(2)}, u32[]{:S(2)}) async-start(bf16[32,128,512]{2,1,0:T(8,128)(2,1)} %bitcast.63), calls=%async_computation | async-start | bytes 8388608 | tf_op jit(solution)/shard_map/all_to_all | solution.py:140
  543.1 152.9 %all-to-all-done = bf16[32,128,512]{2,1,0:T(8,128)(2,1)} async-done(((bf16[32,128,512]{2,1,0:T(8,128)(2,1)}), bf16[32,128,512]{2,1,0:T(8,128)(2,1)}, u32[]{:S(2)}, u32[]{:S(2)}) %all-to-all-start) | async-done | bytes 4194336 | tf_op jit(solution)/shard_map/all_to_all | solution.py:140
  696.0 2.8 reduce_sum.43
  699.6 233.9 %all-gather.8.cloned.1.call-done = bf16[4096,768]{1,0:T(8,128)(2,1)} async-done(((bf16[128,768]{1,0:T(8,128)(2,1)}), bf16[4096,768]{1,0:T(8,128)(2,1)}) %all-gather.8.cloned.1.call-update) | async-done | bytes 6291472 | tf_op jit(solution)/shard_map/all_gather | solution.py:149
  933.5 6.0 convolution_convert_fusion.3
  939.5 137.5 %reduce-scatter.2.cloned.1.call-done = bf16[256,256]{1,0:T(8,128)(2,1)} async-done(((bf16[4096,256]{1,0:T(8,128)(2,1)}), bf16[256,256]{1,0:T(8,128)(2,1)}) %reduce-scatter.2.cloned.1.call-update) | async-done | bytes 131088 | tf_op jit(solution)/shard_map/reduce_scatter | solution.py:151
  (203 shorter events, 38.5 us)
Async XLA Ops:
  6.5 216.9 %all-gather.4.cloned.1.call-start = ((), (), s32[]{:S(2)}) async-start(), calls=%async_computation.2 | async-start | bytes 2162688 | tf_op jit(solution)/shard_map/all_gather | solution.py:70
  7.3 442.8 %all-gather.6.cloned.1.call-start = ((), (), s32[]{:S(2)}) async-start(), calls=%async_computation.3 | async-start | bytes 2162688 | tf_op jit(solution)/shard_map/all_gather | solution.py:71
  511.9 184.1 %all-to-all-start = ((bf16[32,128,512]{2,1,0:T(8,128)(2,1)}), bf16[32,128,512]{2,1,0:T(8,128)(2,1)}, u32[]{:S(2)}, u32[]{:S(2)}) async-start(bf16[32,128,512]{2,1,0:T(8,128)(2,1)} %bitcast.63), calls=%async_computation | async-start | bytes 8388608 | tf_op jit(solution)/shard_map/all_to_all | solution.py:140
  542.8 390.7 %copy-start = (bf16[256,256]{1,0:T(8,128)(2,1)S(1)}, bf16[256,256]{1,0:T(8,128)(2,1)}, u32[]{:S(2)}) copy-start(bf16[256,256]{1,0:T(8,128)(2,1)} %param.25) | copy-start | bytes 393220
  542.8 390.7 %copy-start.1 = (bf16[256,256]{1,0:T(8,128)(2,1)S(1)}, bf16[256,256]{1,0:T(8,128)(2,1)}, u32[]{:S(2)}) copy-start(bf16[256,256]{1,0:T(8,128)(2,1)} %param.24) | copy-start | bytes 393220
  542.8 390.7 %copy-start.2 = (bf16[256,256]{1,0:T(8,128)(2,1)S(1)}, bf16[256,256]{1,0:T(8,128)(2,1)}, u32[]{:S(2)}) copy-start(bf16[256,256]{1,0:T(8,128)(2,1)} %param.23) | copy-start | bytes 393220
  542.8 390.7 %all-gather.8.cloned.1.call-start = ((), (), s32[]{:S(2)}) async-start(), calls=%async_computation.4 | async-start | bytes 6488064 | tf_op jit(solution)/shard_map/all_gather | solution.py:149
  699.6 377.5 %reduce-scatter.2.cloned.1.call-start = ((), (), s32[]{:S(2)}) async-start(), calls=%async_computation.5 | async-start | bytes 2228224 | tf_op jit(solution)/shard_map/reduce_scatter | solution.py:151
Sparse Core Ops, SparseCore 0:
  9.4 213.9 all-gather.3
  225.5 224.5 all-gather.5
  699.7 233.7 all-gather.7
  939.6 137.3 reduce-scatter.1
where the time goes:
time: 1090 us; the launch traced here: 1080 us
  waiting for transfers between devices  928 us (85%)
  local copies, waits for them, and re-layouts  35.5 us (3%)
  starting transfers between devices  31 us (3%)
  other arithmetic  30.4 us (3%)
  matrix products  25.4 us (2%)
  loops' own time  20.1 us (2%)
  between operations  13.3 us (1%)
    all_gather x1, waiting for transfers between devices, per_device(): gradients = lax.all_gather(own_grads, 'ctx', axis=0, tiled=True)  234 us
    all_gather x1, waiting for transfers between devices, per_device(): lax.all_gather(key_states, 'ctx', axis=0, tiled=True)  212 us
    all_gather x1, waiting for transfers between devices, per_device(): lax.all_gather(value_states, 'ctx', axis=0, tiled=True)  190 us
    all_to_all x1, waiting for transfers between devices, per_device(): lax.all_to_all(part_grads.reshape(context_count, slab_rows, part_width),...  153 us
    reduce_scatter x1, waiting for transfers between devices, per_device(): lax.psum_scatter(lax.dot_general(gradients, projections, (((1,), (1,)), (...  138 us
    all_to_all x1, starting transfers between devices, per_device(): lax.all_to_all(part_grads.reshape(context_count, slab_rows, part_width),...  30.9 us
  transfers between devices with their start and end apart: 5, of which 5 were waited for; matrix products, arithmetic and copies ran while one was open for 3% of the time, Pallas kernels for 0%

commit v1 on v0

--- a/solution.py
+++ b/solution.py
@@ -67,7 +67,9 @@
         jnp.zeros((head_count, slab_rows), jnp.float32),
     )
     full_keys, full_values = (
-        lax.all_gather(key_states, "ctx", axis=0, tiled=True),
+        jnp.concatenate(
+            lax.all_to_all(jnp.stack([key_states] * lax.axis_size("ctx")), "ctx", 0, 0), axis=0
+        ),
         lax.all_gather(value_states, "ctx", axis=0, tiled=True),
     )
     group_size = min(context_count, max(1, 512 // slab_rows))

time: 1090 us -> 940 us (0.86)
  the two profiles are of different devices: /device:TPU:2 before, /device:TPU:4 now
where the time goes in v1:
time: 940 us; the launch traced here: 938 us
  waiting for transfers between devices  767 us (82%)
  local copies, waits for them, and re-layouts  41.4 us (4%)
  starting transfers between devices  38 us (4%)
  other arithmetic  31.5 us (3%)
  matrix products  25.4 us (3%)
  loops' own time  21.7 us (2%)
  between operations  13.3 us (1%)
    all_gather x1, waiting for transfers between devices, per_device(): gradients = lax.all_gather(own_grads, 'ctx', axis=0, tiled=True)  235 us
    all_gather x1, waiting for transfers between devices, per_device(): lax.all_gather(value_states, 'ctx', axis=0, tiled=True)  233 us
    all_to_all x1, waiting for transfers between devices, per_device(): lax.all_to_all(part_grads.reshape(context_count, slab_rows, part_width),...  160 us
    reduce_scatter x1, waiting for transfers between devices, per_device(): lax.psum_scatter(lax.dot_general(gradients, projections, (((1,), (1,)), (...  138 us
    all_to_all x1, starting transfers between devices, per_device(): lax.all_to_all(part_grads.reshape(context_count, slab_rows, part_width),...  22.1 us
  transfers between devices with their start and end apart: 5, of which 4 were waited for; matrix products, arithmetic and copies ran while one was open for 1% of the time, Pallas kernels for 0%

profile of v1, /device:TPU:4, one launch (start us, length us, event | category | flops | bytes accessed | tf_op | source)
XLA Modules:
  0.0 938.4 jit_solution(3557537594540027605)
XLA Ops:
  6.5 0.9 copy.67
  7.5 1.8 stack.2
  9.3 15.8 %all-to-all-start = ((bf16[32,128,256]{1,2,0:T(8,128)(2,1)}), bf16[32,128,256]{1,2,0:T(8,128)(2,1)S(1)}, u32[]{:S(2)}, u32[]{:S(2)}) async-start(bf16[32,128,256]{1,2,0:T(8,128)(2,1)} %stack.2), calls=%async_computation | async-start | bytes 4194304 | tf_op jit(solution)/shard_map/all_to_all | solution.py:71
  26.4 233.4 %all-gather.3.cloned.1.call-done = bf16[4096,256]{1,0:T(8,128)(2,1)} async-done(((bf16[128,256]{1,0:T(8,128)(2,1)}), bf16[4096,256]{1,0:T(8,128)(2,1)}) %all-gather.3.cloned.1.call-update) | async-done | bytes 2097168 | tf_op jit(solution)/shard_map/all_gather | solution.py:73
  259.9 4.0 reshape.82
  263.8 3.3 copy.76
  267.2 2.7 copy.68
  269.9 4.4 reshape_reshape.6
  274.2 3.5 copy.75
  277.7 32.7 %while.33 = (s32[]{:T(128)}, f32[2,128]{1,0:T(2,128)S(1)}, f32[2,128]{1,0:T(2,128)S(1)}, s32[8]{0:T(128)S(1)}, s32[32,32]{1,0:T(8,128)}, /*index=5*/s32[]{:T(128...) while((s32[]{:T(128)}, f32[2,128]{1,0:T(2,128)S(1)}, ...), condition=%wide.region_6.7_spmd, body=%wide.region_0.6_spmd.sunk | while | flops 34406940 | bytes 1391623 | solution.py:94
  279.1 0.8 broadcast_compare_fusion.6
  279.8 0.8 broadcast_reduce_fusion.4
  283.1 0.8 broadcast_compare_fusion.6
  283.9 0.8 broadcast_reduce_fusion.4
  287.2 0.8 broadcast_compare_fusion.6
  288.0 0.8 broadcast_reduce_fusion.4
  291.3 0.8 broadcast_compare_fusion.6
  292.1 0.8 broadcast_reduce_fusion.4
  295.4 0.8 broadcast_compare_fusion.6
  296.2 0.8 broadcast_reduce_fusion.4
  300.3 0.8 broadcast_reduce_fusion.4
  304.4 0.8 broadcast_reduce_fusion.4
  308.5 0.8 broadcast_reduce_fusion.4
  310.5 56.4 %while.34 = (s32[]{:T(128)}, f32[128,2,128]{2,0,1:T(8,128)S(1)}, bf16[8,512,512]{2,1,0:T(8,128)(2,1)}, s32[8]{0:T(128)S(1)}, s32[32,32]{1,0:T(8,128)}, /*index=5...) while((s32[]{:T(128)}, f32[128,2,128]{2,0,1:T(8,128)S(1)}, ...), condition=%wide.region_13.14_spmd, body=%wide.region_8.13_spmd.sunk | while | flops 170721312 | bytes 8655399 | solution.py:134
  311.8 0.8 broadcast_compare_fusion.7
  312.6 0.8 broadcast_reduce_fusion.5
  314.1 2.5 conditional.5
  314.5 1.2 fusion.11
  316.8 0.8 constant_dynamic-update-slice_fusion.2
  318.9 0.8 broadcast_compare_fusion.7
  319.7 0.8 broadcast_reduce_fusion.5
  321.1 2.5 conditional.5
  321.5 1.2 fusion.11
  323.8 0.8 constant_dynamic-update-slice_fusion.2
  326.7 0.8 broadcast_reduce_fusion.5
  328.2 2.5 conditional.5
  328.6 1.2 fusion.11
  330.9 0.8 constant_dynamic-update-slice_fusion.2
  333.8 0.8 broadcast_reduce_fusion.5
  335.2 2.5 conditional.5
  335.6 1.2 fusion.11
  337.9 0.8 constant_dynamic-update-slice_fusion.2
  340.8 0.8 broadcast_reduce_fusion.5
  342.3 2.5 conditional.5
  342.7 1.2 fusion.11
  345.0 0.8 constant_dynamic-update-slice_fusion.2
  347.9 0.8 broadcast_reduce_fusion.5
  349.3 2.5 conditional.5
  349.7 1.2 fusion.11
  352.0 0.8 constant_dynamic-update-slice_fusion.2
  354.9 0.8 broadcast_reduce_fusion.5
  356.4 2.5 conditional.5
  356.8 1.2 fusion.11
  359.1 0.8 constant_dynamic-update-slice_fusion.2
  362.0 0.8 broadcast_reduce_fusion.5
  363.4 2.5 conditional.5
  363.8 1.2 fusion.11
  366.1 0.8 constant_dynamic-update-slice_fusion.2
  367.0 22.1 %all-to-all-start.1 = ((bf16[32,128,512]{2,1,0:T(8,128)(2,1)}), bf16[32,128,512]{2,1,0:T(8,128)(2,1)}, u32[]{:S(2)}, u32[]{:S(2)}) async-start(bf16[32,128,512]{2,1,0:T(8,128)(2,1)} %bitcast.65), calls=%async_computation.1 | async-start | bytes 8388608 | tf_op jit(solution)/shard_map/all_to_all | solution.py:142
  389.4 160.4 %all-to-all-done.1 = bf16[32,128,512]{2,1,0:T(8,128)(2,1)} async-done(((bf16[32,128,512]{2,1,0:T(8,128)(2,1)}), bf16[32,128,512]{2,1,0:T(8,128)(2,1)}, u32[]{:S(2)}, u32[]{:S(2)}) %all-to-all-start.1) | async-done | bytes 4194336 | tf_op jit(solution)/shard_map/all_to_all | solution.py:142
  549.8 2.8 reduce_sum.43
  553.3 234.8 %all-gather.5.cloned.1.call-done = bf16[4096,768]{1,0:T(8,128)(2,1)} async-done(((bf16[128,768]{1,0:T(8,128)(2,1)}), bf16[4096,768]{1,0:T(8,128)(2,1)}) %all-gather.5.cloned.1.call-update) | async-done | bytes 6291472 | tf_op jit(solution)/shard_map/all_gather | solution.py:151
  788.2 6.0 convolution_convert_fusion.3
  794.2 137.7 %reduce-scatter.2.cloned.1.call-done = bf16[256,256]{1,0:T(8,128)(2,1)} async-done(((bf16[4096,256]{1,0:T(8,128)(2,1)}), bf16[256,256]{1,0:T(8,128)(2,1)}) %reduce-scatter.2.cloned.1.call-update) | async-done | bytes 131088 | tf_op jit(solution)/shard_map/reduce_scatter | solution.py:153
  (211 shorter events, 39.3 us)
Async XLA Ops:
  9.3 16.6 %copy-start.1 = (bf16[128,256]{1,0:T(8,128)(2,1)S(1)}, bf16[128,256]{1,0:T(8,128)(2,1)}, u32[]{:S(2)}) copy-start(bf16[128,256]{1,0:T(8,128)(2,1)} %param.17) | copy-start | bytes 196612
  9.3 16.8 %copy-start.2 = (bf16[128,256]{1,0:T(8,128)(2,1)S(1)}, bf16[128,256]{1,0:T(8,128)(2,1)}, u32[]{:S(2)}) copy-start(bf16[128,256]{1,0:T(8,128)(2,1)} %param.21) | copy-start | bytes 196612
  9.3 17.0 %copy-start = (bf16[128,256]{1,0:T(8,128)(2,1)S(1)}, bf16[128,256]{1,0:T(8,128)(2,1)}, u32[]{:S(2)}) copy-start(bf16[128,256]{1,0:T(8,128)(2,1)} %param.20) | copy-start | bytes 196612
  9.3 257.8 %all-to-all-start = ((bf16[32,128,256]{1,2,0:T(8,128)(2,1)}), bf16[32,128,256]{1,2,0:T(8,128)(2,1)S(1)}, u32[]{:S(2)}, u32[]{:S(2)}) async-start(bf16[32,128,256]{1,2,0:T(8,128)(2,1)} %stack.2), calls=%async_computation | async-start | bytes 4194304 | tf_op jit(solution)/shard_map/all_to_all | solution.py:71
  25.1 234.7 %all-gather.3.cloned.1.call-start = ((), (), s32[]{:S(2)}) async-start(), calls=%async_computation.3 | async-start | bytes 2162688 | tf_op jit(solution)/shard_map/all_gather | solution.py:73
  367.0 182.8 %all-to-all-start.1 = ((bf16[32,128,512]{2,1,0:T(8,128)(2,1)}), bf16[32,128,512]{2,1,0:T(8,128)(2,1)}, u32[]{:S(2)}, u32[]{:S(2)}) async-start(bf16[32,128,512]{2,1,0:T(8,128)(2,1)} %bitcast.65), calls=%async_computation.1 | async-start | bytes 8388608 | tf_op jit(solution)/shard_map/all_to_all | solution.py:142
  389.1 399.1 %all-gather.5.cloned.1.call-start = ((), (), s32[]{:S(2)}) async-start(), calls=%async_computation.4 | async-start | bytes 6488064 | tf_op jit(solution)/shard_map/all_gather | solution.py:151
  389.4 398.8 %copy-start.3 = (bf16[256,256]{1,0:T(8,128)(2,1)S(1)}, bf16[256,256]{1,0:T(8,128)(2,1)}, u32[]{:S(2)}) copy-start(bf16[256,256]{1,0:T(8,128)(2,1)} %param.25) | copy-start | bytes 393220
  389.4 398.8 %copy-start.4 = (bf16[256,256]{1,0:T(8,128)(2,1)S(1)}, bf16[256,256]{1,0:T(8,128)(2,1)}, u32[]{:S(2)}) copy-start(bf16[256,256]{1,0:T(8,128)(2,1)} %param.24) | copy-start | bytes 393220
  389.4 398.8 %copy-start.5 = (bf16[256,256]{1,0:T(8,128)(2,1)S(1)}, bf16[256,256]{1,0:T(8,128)(2,1)}, u32[]{:S(2)}) copy-start(bf16[256,256]{1,0:T(8,128)(2,1)} %param.23) | copy-start | bytes 393220
  553.3 378.6 %reduce-scatter.2.cloned.1.call-start = ((), (), s32[]{:S(2)}) async-start(), calls=%async_computation.5 | async-start | bytes 2228224 | tf_op jit(solution)/shard_map/reduce_scatter | solution.py:153
Sparse Core Ops, SparseCore 0:
  28.0 231.7 all-gather.2
  553.4 234.6 all-gather.4
  794.3 137.5 reduce-scatter.1
